TPU v7x, 512 devices: a whole 4x8x8 slice. The times are simulated.
512 devices in a mesh: row: 32 (over z, x), col: 16 (over y, core).
Axes of the slice: x: 4, y: 8, z: 8, core: 2. Of those that a mesh axis runs over, the one named last changes fastest.
Arguments:
- features: float32 [24576, 64], P('row'), may hold values from -6 to 6
- noise: float32 [24576], P('row'), may hold values from 0.1 to 1
- tile_map: int32 [192], replicated, may hold values from 0 to 191, each once
- panel_tile: int32 [1], replicated, may hold values from 0 to 143
Outputs:
- panel: float32 [24576, 128], P('row')
- trailing: float32 [24576, 24576], P('row', 'col')
Inputs may be any that keep to these rules, and one draw needn't show every extreme that they name: `tile_map`: a permutation: every global tile 0 to 191 is held by exactly one slot.
All inputs are finite; a program needn't handle non-finite values.
Results may differ from a plain program's by a relative error of at most 0.0003.
Values sent between devices are 32-bit elements; how exact they have to be, the bound alone decides.
No kernel may reach another device: no remote copies, remote signals or barrier semaphores. Data moves between devices by JAX's collectives and lax.ppermute only.
A program may use at most 64 MiB of HBM per device.

v0:
```python
import jax
import jax.numpy as jnp
from jax import lax
from jax.sharding import PartitionSpec as P

TILE = 128


HIGHEST_MODE = lax.Precision.HIGHEST


def broadcast(block, axis, holder):
    block = jnp.where(lax.axis_index(axis) == holder, block, jnp.zeros_like(block))
    return lax.psum(block, axis)


def kernel_block(left_rows, right_rows):
    inner_part = jnp.dot(
        left_rows, right_rows.T, precision=HIGHEST_MODE, preferred_element_type=jnp.float32
    )
    left_sq = jnp.sum(left_rows * left_rows, axis=1)
    right_sq = jnp.sum(right_rows * right_rows, axis=1)
    return jnp.exp((2.0 * inner_part - left_sq[:, None] - right_sq[None, :]) / left_rows.shape[1])


def pivot_inverse(pivot_feat, pivot_noise):
    kernel_part = kernel_block(pivot_feat, pivot_feat) + jnp.diag(pivot_noise)
    lower_factor = jnp.linalg.cholesky(kernel_part)
    identity = jnp.eye(kernel_part.shape[0], dtype=kernel_part.dtype)
    return jax.scipy.linalg.solve_triangular(lower_factor, identity, lower=True)


def panel_piece(feat_rows, noise_rows, tile_of_row, offset_of_row, pivot_feat, inverse, pivot_tile):
    tile_width = pivot_feat.shape[0]
    kernel_part = kernel_block(feat_rows, pivot_feat)
    on_diagonal = (tile_of_row == pivot_tile)[:, None] & (
        offset_of_row[:, None] == jnp.arange(tile_width, dtype=jnp.int32)[None, :]
    )
    kernel_part = kernel_part + jnp.where(on_diagonal, noise_rows[:, None], 0.0)
    factor = jnp.dot(
        kernel_part, inverse.T, precision=HIGHEST_MODE, preferred_element_type=jnp.float32
    )
    return jnp.where((tile_of_row >= pivot_tile)[:, None], factor, 0.0)


def trailing_block(
    row_feat,
    row_noise,
    row_panel,
    row_tile,
    row_offset,
    col_feat,
    col_panel,
    col_tile,
    col_offset,
    pivot_tile,
):
    kernel_part = kernel_block(row_feat, col_feat)
    same_entry = (row_tile[:, None] == col_tile[None, :]) & (
        row_offset[:, None] == col_offset[None, :]
    )
    kernel_part = kernel_part + jnp.where(same_entry, row_noise[:, None], 0.0)
    kernel_part = kernel_part - jnp.dot(
        row_panel, col_panel.T, precision=HIGHEST_MODE, preferred_element_type=jnp.float32
    )
    live_entry = (row_tile[:, None] >= col_tile[None, :]) & (col_tile[None, :] > pivot_tile)
    return jnp.where(live_entry, kernel_part, 0.0)


def shards(features, noise, tile_map, panel_tile):
    tile_width = TILE
    rows_here = features.shape[0]
    tiles_here = rows_here // tile_width
    blocks_per_col = lax.axis_size("row") // lax.axis_size("col")
    row_index = lax.axis_index("row")
    col_index = lax.axis_index("col")
    tile_count = tile_map.shape[0]
    pivot_tile = panel_tile[0]
    slot_ids = jnp.arange(tile_count, dtype=jnp.int32)
    pivot_slot = jnp.sum(jnp.where(tile_map == pivot_tile, slot_ids, 0))
    local_slot = jnp.clip(pivot_slot - row_index * tiles_here, 0, tiles_here - 1)
    own_feat = lax.dynamic_slice_in_dim(features, local_slot * tile_width, tile_width, 0)
    own_noise = lax.dynamic_slice_in_dim(noise, local_slot * tile_width, tile_width, 0)
    pivot_feat, pivot_noise = (
        broadcast(own_feat, "row", pivot_slot // tiles_here),
        broadcast(own_noise, "row", pivot_slot // tiles_here),
    )
    inverse = pivot_inverse(pivot_feat, pivot_noise)
    row_tiles = lax.dynamic_slice_in_dim(tile_map, row_index * tiles_here, tiles_here, 0)
    tile_of_row = jnp.repeat(row_tiles, tile_width)
    offset_of_row = jnp.tile(jnp.arange(tile_width, dtype=jnp.int32), tiles_here)
    panel_rows = panel_piece(
        features, noise, tile_of_row, offset_of_row, pivot_feat, inverse, pivot_tile
    )
    col_tiles = lax.dynamic_slice_in_dim(
        tile_map, col_index * tiles_here * blocks_per_col, tiles_here * blocks_per_col, 0
    )
    tile_of_col = jnp.repeat(col_tiles, tile_width)
    offset_of_col = jnp.tile(jnp.arange(tile_width, dtype=jnp.int32), tiles_here * blocks_per_col)
    feat_parts = []
    panel_parts = []
    for member in range(blocks_per_col):
        got_panel, got_feat = (
            broadcast(panel_rows, "row", col_index * blocks_per_col + member),
            broadcast(features, "row", col_index * blocks_per_col + member),
        )
        panel_parts.append(got_panel)
        feat_parts.append(got_feat)
    col_feat = jnp.concatenate(feat_parts, axis=0)
    col_panel = jnp.concatenate(panel_parts, axis=0)
    trailing = trailing_block(
        features,
        noise,
        panel_rows,
        tile_of_row,
        offset_of_row,
        col_feat,
        col_panel,
        tile_of_col,
        offset_of_col,
        pivot_tile,
    )
    return (panel_rows, trailing)


def solution(mesh):
    in_specs = (P("row", None), P("row"), P(), P())
    out_specs = (P("row", None), P("row", "col"))
    return jax.shard_map(shards, mesh=mesh, in_specs=in_specs, out_specs=out_specs, check_vma=False)
```

profile of v0, /device:TPU:56, one launch (start us, length us, event | category | flops | bytes accessed | tf_op | source)
XLA Modules:
  0.0 376.0 jit_solution(8831978693632658781)
XLA Ops:
  7.2 0.0 copy-start.2
  7.2 0.0 all-reduce.4.cloned.1.call-start
  7.9 1.3 fusion.22
  11.8 0.8 dynamic_slice.12
  12.6 0.8 broadcast_select_fusion.4
  13.4 0.8 dynamic-slice_select_fusion
  14.1 148.9 %all-reduce = (f32[128,64]{0,1:T(8,128)S(1)}, f32[128]{0:T(128)S(1)}) all-reduce(f32[128,64]{0,1:T(8,128)S(1)} %dynamic-slice_select_fusion, f32[128]{0:T(128)S(1)} %broadcast_select_fusion.4), channel_id=1, replica_groups=mesh['row'=32,'col'=16] {'row'}, use_global_device_ids=true, to_apply=%region_1.2 | all-reduce | flops 8320 | bytes 66560 | tf_op jit(solution)/shard_map/psum | solution.py:14
  163.0 0.3 fusion.11
  163.3 0.1 copy.7
  163.4 0.1 fusion.21
  163.5 11.7 %cholesky.17 = f32[128,128]{1,0:T(8,128)S(1)} custom-call(f32[128,128]{1,0:T(8,128)S(1)} %fusion.21), custom_call_target="Cholesky" | custom-call | tf_op jit(solution)/shard_map/jit(cholesky)/cholesky | solution.py:28
  175.3 0.6 compare_reduce_fusion
  175.9 0.7 fusion.17
  176.6 9.8 %custom-call.7 = f32[1,128,128]{1,2,0:T(8,128)S(1)} custom-call(f32[1,128,128]{2,1,0:T(8,128)S(1)} %fusion.17), custom_call_target="InvertDiagBlocksLowerTriangular" | custom-call | tf_op jit(solution)/shard_map/jit(_solve_triangular)/triangular_solve | solution.py:30
  186.4 0.2 fusion.18
  186.6 0.1 bitcast_compare_fusion.2
  186.7 1.7 broadcast_select_fusion.2
  188.4 2.6 fusion.7
  191.1 1.4 broadcast_select_fusion.1
  192.4 0.0 all-reduce.4.cloned.1.call-update
  192.5 0.1 dynamic_slice.15
  192.5 0.1 bitcast_compare_fusion
  192.6 0.1 broadcast_bitcast_fusion.1
  192.7 0.1 iota_bitcast_fusion
  192.8 154.9 %all-reduce.4.cloned.1.call-done = (f32[768,128]{1,0:T(8,128)}, f32[768,128]{1,0:T(8,128)}, f32[768,64]{0,1:T(8,128)}, f32[768,64]{0,1:T(8,128)}) async-done(((f32[768,128]{1,0:T(8,128)}, f32[768,128]{1,0:T(8,128)}, f32[768,64]{0,1:T(8,128)}, f32[768,64]{0,1:T(8,128)}), (f32[768,128]{1,0:T(8,128)}, f32[768,128]{1,0:T(8,128)}, f32[768,64]{0,1:T(8,128)}, f32[768,64]{0,1:T(8,128)})) %all-reduce.4.cloned.1.call-update) | async-done | bytes 1179664 | tf_op jit(solution)/shard_map/psum | solution.py:14
  347.7 0.9 constant_dynamic-update-slice_fusion.1
  348.6 0.9 constant_dynamic-update-slice_fusion
  349.6 0.0 copy-start.1
  349.6 0.0 copy-start.3
  349.7 5.2 %fusion.12 = f32[768,1536]{0,1:T(8,128)S(1)} fusion(f32[768,128]{1,0:T(8,128)S(1)} %get-tuple-element.17, f32[768,128]{1,0:T(8,128)} %get-tuple-element.6, f32[768,128]{1,0:T(8,128)} %get-tuple-element.7), kind=kOutput, calls=%fused_computation.16 | convolution fusion | flops 1812135936 | bytes 5898240 | tf_op jit(solution)/shard_map/dot_general | solution.py:63
  354.9 8.2 %fusion.1 = f32[768,1536]{0,1:T(8,128)} fusion(f32[768,1536]{0,1:T(8,128)S(1)} %fusion.12, f32[1536,64]{0,1:T(8,128)S(1)} %constant_dynamic-update-slice_fusion, f32[768,64]{0,1:T(8,128)S(1)} %copy-done.1, f32[768]{0:T(1024)S(1)} %copy-done.3, s32[768]{0:T(1024)S(1)} %iota_bitcast_fusion.1, f32[1536]{0:T(1024)S(1)} %multiply_reduce_fusion, ...), kind=kOutput, calls=%fused_computation.2 | convolution fusion | flops 921305088 | bytes 10059264 | tf_op jit(solution)/shard_map/dot_general | solution.py:18
  363.1 6.0 %copy.9 = f32[768,1536]{1,0:T(8,128)} copy(f32[768,1536]{0,1:T(8,128)} %fusion.1) | data formatting | bytes 9437184
  (9 shorter events, 0.1 us)
Async XLA Ops:
  7.2 185.3 %copy-start.2 = (s32[192]{0:T(256)S(1)}, s32[192]{0:T(256)}, u32[]{:S(2)}) copy-start(s32[192]{0:T(256)} %param.6) | copy-start | bytes 2308
  7.2 340.5 %all-reduce.4.cloned.1.call-start = ((), (), s32[]{:S(2)}) async-start(), calls=%async_computation | async-start | bytes 2359296 | tf_op jit(solution)/shard_map/psum | solution.py:14
  192.4 162.5 %copy-start = (f32[768,128]{1,0:T(8,128)}, f32[768,128]{1,0:T(8,128)S(1)}, u32[]{:S(2)}) copy-start(f32[768,128]{1,0:T(8,128)S(1)} %get-tuple-element.17) | copy-start | bytes 1179652
  349.6 5.2 %copy-start.1 = (f32[768,64]{0,1:T(8,128)S(1)}, f32[768,64]{0,1:T(8,128)}, u32[]{:S(2)}) copy-start(f32[768,64]{0,1:T(8,128)} %param.4) | copy-start | bytes 589828
  349.6 5.2 %copy-start.3 = (f32[768]{0:T(1024)S(1)}, f32[768]{0:T(1024)}, u32[]{:S(2)}) copy-start(f32[768]{0:T(1024)} %param.5) | copy-start | bytes 9220
Sparse Core Ops, SparseCore 0:
  192.6 155.0 all-reduce.3
where the time goes:
time: 377 us; the launch traced here: 376 us
  waiting for transfers between devices  155 us (41%)
  blocking collectives  149 us (40%)
  other arithmetic  27.7 us (7%)
  matrix products  18 us (5%)
  between operations  17.5 us (5%)
  local copies, waits for them, and re-layouts  9.01 us (2%)
    psum x1, waiting for transfers between devices, broadcast(): return lax.psum(block, axis)  155 us
    psum x1, blocking collectives, broadcast(): return lax.psum(block, axis)  149 us
    another operation x3, other arithmetic, pivot_inverse(): lower_factor = jnp.linalg.cholesky(kernel_part)  12.4 us
    dot_general x3, matrix products, kernel_block(): jnp.dot(left_rows, right_rows.T, precision=HIGHEST_MODE, preferred_elemen...  11.2 us
    another operation x2, other arithmetic, pivot_inverse(): return jax.scipy.linalg.solve_triangular(lower_factor, identity, lower=True)  10.5 us
  transfers between devices with their start and end apart: 1, of which 1 were waited for; matrix products, arithmetic and copies ran while one was open for 0% of the time, Pallas kernels for 0%

commit v1 on v0

v1 whole, which is shorter than its diff:
```python
import jax
import jax.numpy as jnp
from jax import lax
from jax.experimental import pallas as pl
from jax.experimental.pallas import tpu as pltpu
from jax.sharding import PartitionSpec as P

TILE = 128
FEAT = 64
HIGHEST_MODE = lax.Precision.HIGHEST
F32 = jnp.float32
BF16 = jnp.bfloat16
VMEM = pltpu.VMEM
SMEM = pltpu.SMEM
CHUNK = 256


def vspec():
    return pl.BlockSpec(memory_space=VMEM)


def sspec():
    return pl.BlockSpec(memory_space=SMEM)


def pivot_slot_of(map_ref, panel_ref, tile_count):
    pivot = panel_ref[0]

    def step(s, slot):
        return jnp.where(map_ref[s] == pivot, s, slot)

    return lax.fori_loop(0, tile_count, step, jnp.int32(0), unroll=16)


def pack_kernel(tiles_here, map_ref, panel_ref, feat_ref, noise_ref, out_ref, slot_ref):
    slot = pivot_slot_of(map_ref, panel_ref, map_ref.shape[0])
    slot_ref[0] = slot
    local = jnp.clip(slot - lax.axis_index("row") * tiles_here, 0, tiles_here - 1)
    rows = feat_ref.shape[1]
    extra = jnp.broadcast_to(noise_ref[pl.ds(local, 1), :], (2, TILE))
    for r in range(out_ref.shape[0]):
        out_ref[r, :, :rows] = feat_ref[2 * r : 2 * r + 2, :]
        out_ref[r, :, rows:] = extra


def pick_kernel(tiles_here, blocks_per_col, slot_ref, got_ref, out_ref, noise_ref):
    slot = slot_ref[0]
    rows = tiles_here * TILE
    first = lax.axis_index("col") * blocks_per_col
    owner = slot // tiles_here
    offset = pl.multiple_of((slot - owner * tiles_here) * TILE, TILE)
    noise_ref[...] = got_ref[owner, 0:1, rows:]
    parts = [got_ref[first + m, :, :rows] for m in range(blocks_per_col)]
    parts.append(got_ref[owner, :, pl.ds(offset, TILE)])
    for r in range(out_ref.shape[0]):
        at = 0
        for part in parts:
            out_ref[r, :, at : at + part.shape[1]] = part
            at += part.shape[1]


def split2(x):
    hi = x.astype(BF16).astype(F32)
    return hi, x - hi


def split3(x):
    a = x.astype(BF16).astype(F32)
    b = (x - a).astype(BF16).astype(F32)
    return a, b, x - a - b


def tail(norm, mine_first):
    n = norm.shape[1]
    at = lax.broadcasted_iota(jnp.int32, (16, n), 0)
    a, b, c = (jnp.broadcast_to(-v, (16, n)) for v in split3(norm))
    base = 0 if mine_first else 3
    out = jnp.where((at >= 3 - base) & (at < 6 - base), 1.0, 0.0)
    for i, v in enumerate((a, b, c)):
        out = jnp.where(at == base + i, v, out)
    return out


def left_side(feat_t):
    norm = jnp.sum(feat_t * feat_t, axis=0, keepdims=True) * (1.0 / FEAT)
    hi, lo = split2(feat_t)
    return jnp.concatenate([hi, hi, lo, tail(norm, True)], axis=0)


def right_side(feat_t):
    norm = jnp.sum(feat_t * feat_t, axis=0, keepdims=True) * (1.0 / FEAT)
    hi, lo = split2(feat_t * (2.0 / FEAT))
    return jnp.concatenate([hi, lo, hi, tail(norm, False)], axis=0).astype(BF16)


def inverse_factor(gram, inv_ref):
    w = [gram[8 * t : 8 * t + 8, :] for t in range(TILE // 8)]
    lane = lax.broadcasted_iota(jnp.int32, (1, TILE), 1)
    sub = lax.broadcasted_iota(jnp.int32, (8, 1), 0)
    for j in range(TILE):
        jt, js = divmod(j, 8)
        row = w[jt][js : js + 1, :]
        piv = row[:, j : j + 1]
        scaled = jnp.where(lane == j, piv + 1.0, row) * (1.0 / piv)
        inv_ref[j : j + 1, :] = jnp.where(
            lane < j, row, jnp.where(lane == j, 1.0, 0.0)
        ) * lax.rsqrt(piv)
        for t in range(jt, TILE // 8):
            col = w[t][:, j : j + 1]
            if t == jt:
                if js == 7:
                    continue
                col = jnp.where(sub > js, col, 0.0)
            w[t] = w[t] - col * scaled


def dot(a, b, precision=None):
    return jnp.dot(a, b, precision=precision, preferred_element_type=F32)


def step_kernel(
    tiles_here,
    map_ref,
    panel_tile_ref,
    slot_ref,
    got_ref,
    pivot_noise_ref,
    feat_ref,
    noise_ref,
    panel_ref,
    out_ref,
    all_t,
    inv_ref,
    left_ref,
    right_ref,
    row_panel_ref,
    col_panel_ref,
):
    chunk = pl.program_id(0)
    rows = tiles_here * TILE
    cols = right_ref.shape[1]
    tiles_across = cols // TILE
    slot = slot_ref[0]
    pivot = panel_tile_ref[0]
    first_row_slot = lax.axis_index("row") * tiles_here
    first_col_slot = lax.axis_index("col") * tiles_across
    at_row = lax.broadcasted_iota(jnp.int32, (TILE, TILE), 0)
    at_col = lax.broadcasted_iota(jnp.int32, (TILE, TILE), 1)
    diagonal = at_row == at_col

    @pl.when(chunk == 0)
    def _():
        for r in range(got_ref.shape[0]):
            all_t[2 * r : 2 * r + 2, :] = got_ref[r]
        pivot_t = all_t[:, cols:]
        pivot_norm = jnp.sum(pivot_t * pivot_t, axis=0, keepdims=True)
        pivot_rows = pivot_t.T
        pivot_norm_col = jnp.sum(pivot_rows * pivot_rows, axis=1, keepdims=True)
        inner = dot(pivot_rows, pivot_t, HIGHEST_MODE)
        gram = jnp.exp((2.0 * inner - pivot_norm_col - pivot_norm) * (1.0 / FEAT))
        pivot_noise = jnp.where(diagonal, pivot_noise_ref[...], 0.0)
        inverse_factor(gram + pivot_noise, inv_ref)
        inverse = inv_ref[...]
        inverse_t = inverse.T
        pivot_left = left_side(pivot_t).T.astype(BF16)
        pivot_right = right_side(pivot_t)
        right = right_side(all_t[:, :cols])
        right_ref[...] = right
        for j in range(tiles_across):
            here = slice(j * TILE, (j + 1) * TILE)
            kern = jnp.exp(dot(pivot_left, right[:, here]))
            kern = kern + jnp.where(first_col_slot + j == slot, pivot_noise, 0.0)
            hi, lo = split2(dot(inverse, kern, HIGHEST_MODE))
            col_panel_ref[:, here] = jnp.concatenate([hi, lo, hi], axis=0).astype(BF16)
        for i in range(tiles_here):
            here = slice(i * TILE, (i + 1) * TILE)
            left = left_side(feat_ref[:, here]).T.astype(BF16)
            left_ref[here, :] = left
            kern = jnp.exp(dot(left, pivot_right))
            kern = kern + jnp.where(first_row_slot + i == slot, pivot_noise, 0.0)
            factor = dot(kern, inverse_t, HIGHEST_MODE)
            factor = jnp.where(map_ref[first_row_slot + i] >= pivot, factor, 0.0)
            panel_ref[here, :] = factor
            hi, lo = split2(factor)
            row_panel_ref[here, :] = jnp.concatenate([hi, hi, lo], axis=1).astype(BF16)

    across = pl.ds(pl.multiple_of(chunk * CHUNK, CHUNK), CHUNK)
    right = right_ref[:, across]
    col_panel = col_panel_ref[:, across]
    per_chunk = CHUNK // TILE
    for i in range(tiles_here):
        here = slice(i * TILE, (i + 1) * TILE)
        value = jnp.exp(dot(left_ref[here, :], right)) - dot(row_panel_ref[here, :], col_panel)
        row_tile = map_ref[first_row_slot + i]
        for h in range(per_chunk):
            col_slot = first_col_slot + chunk * per_chunk + h
            col_tile = map_ref[col_slot]
            live = (row_tile >= col_tile) & (col_tile > pivot)
            part = slice(h * TILE, (h + 1) * TILE)
            out_ref[here, part] = jnp.where(live, value[:, part], 0.0)

            @pl.when((first_row_slot + i == col_slot) & live)
            def _():
                out_ref[here, part] += jnp.where(diagonal, noise_ref[i : i + 1, :], 0.0)


def shards(features, noise, tile_map, panel_tile):
    rows_here = features.shape[0]
    tiles_here = rows_here // TILE
    members = lax.axis_size("row")
    blocks_per_col = members // lax.axis_size("col")
    cols = rows_here * blocks_per_col
    feat_t = features.T
    noise_2d = noise.reshape(tiles_here, TILE)
    shape = jax.ShapeDtypeStruct
    packed, slot = pl.pallas_call(
        lambda *refs: pack_kernel(tiles_here, *refs),
        out_shape=(shape((members, 2, rows_here + TILE), F32), shape((1,), jnp.int32)),
        in_specs=[sspec(), sspec(), vspec(), vspec()],
        out_specs=(vspec(), sspec()),
        name="pack",
    )(tile_map, panel_tile, feat_t, noise_2d)
    got = lax.all_to_all(packed, "row", 0, 0, tiled=True)
    picked, pivot_noise = pl.pallas_call(
        lambda *refs: pick_kernel(tiles_here, blocks_per_col, *refs),
        out_shape=(shape((members, 2, cols + TILE), F32), shape((1, TILE), F32)),
        in_specs=[sspec(), vspec()],
        out_specs=(vspec(), vspec()),
        name="pick",
    )(slot, got)
    gathered = lax.all_to_all(picked, "row", 0, 0, tiled=True)
    depth = 3 * FEAT + 16
    panel, trailing = pl.pallas_call(
        lambda *refs: step_kernel(tiles_here, *refs),
        grid=(cols // CHUNK,),
        out_shape=(shape((rows_here, TILE), F32), shape((rows_here, cols), F32)),
        in_specs=[sspec(), sspec(), sspec(), vspec(), vspec(), vspec(), vspec()],
        out_specs=(
            pl.BlockSpec((rows_here, TILE), lambda j: (0, 0)),
            pl.BlockSpec((rows_here, CHUNK), lambda j: (0, j)),
        ),
        scratch_shapes=[
            VMEM((FEAT, cols + TILE), F32),
            VMEM((TILE, TILE), F32),
            VMEM((rows_here, depth), BF16),
            VMEM((depth, cols), BF16),
            VMEM((rows_here, 3 * TILE), BF16),
            VMEM((3 * TILE, cols), BF16),
        ],
        compiler_params=pltpu.CompilerParams(vmem_limit_bytes=32 * 1024 * 1024),
        name="step",
    )(tile_map, panel_tile, slot, gathered, pivot_noise, feat_t, noise_2d)
    return panel, trailing


def solution(mesh):
    in_specs = (P("row", None), P("row"), P(), P())
    out_specs = (P("row", None), P("row", "col"))
    return jax.shard_map(shards, mesh=mesh, in_specs=in_specs, out_specs=out_specs, check_vma=False)
```

time: 377 us -> 79.3 us (0.21)
  waiting for transfers between devices: 155 us -> 0 us
  blocking collectives: 149 us -> 44.6 us
  Pallas kernels: 0 us -> 30.1 us
  other arithmetic: 27.7 us -> 0 us
  matrix products: 18 us -> 0 us
  between operations: 17.5 us -> 1.29 us
  local copies, waits for them, and re-layouts: 9.01 us -> 2.95 us
    psum x1 -> x0, waiting for transfers between devices: 155 us -> none  [broadcast(): return lax.psum(block, axis)]
    psum x1 -> x0, blocking collectives: 149 us -> none  [broadcast(): return lax.psum(block, axis)]
    all_to_all x0 -> x2, blocking collectives: none -> 44.6 us  [the longest x1 25.4 us: shards(): got = lax.all_to_all(packed, 'row', 0, 0, tiled=True)]
    pallas_call x0 -> x3, Pallas kernels: none -> 30.1 us  [the longest x1 25.7 us: shards(): pl.pallas_call(lambda *refs: step_kernel(tiles_here, *refs), grid=(cols /...]
    another operation x5 -> x0, other arithmetic: 22.9 us -> none  [the longest x3 12.4 us: pivot_inverse(): lower_factor = jnp.linalg.cholesky(kernel_part)]
    dot_general x5 -> x0, matrix products: 17.7 us -> none  [the longest x3 11.2 us: kernel_block(): jnp.dot(left_rows, right_rows.T, precision=HIGHEST_MODE, preferred_elemen...]
    unnamed x10 -> x8, local copies, waits for them, and re-layouts: 7 us -> 2.95 us
  transfers between devices with their start and end apart: 1 -> 0, of which waited for: 1 -> 0; matrix products, arithmetic and copies ran while one was open for 0% -> 0% of each run, Pallas kernels for 0% -> 0%
where the time goes in v1:
time: 79.3 us; the launch traced here: 78.9 us
  blocking collectives  44.6 us (56%)
  Pallas kernels  30.1 us (38%)
  local copies, waits for them, and re-layouts  2.95 us (4%)
  between operations  1.29 us (2%)
    pallas_call x1, Pallas kernels, shards(): pl.pallas_call(lambda *refs: step_kernel(tiles_here, *refs), grid=(cols /...  25.7 us
    all_to_all x1, blocking collectives, shards(): got = lax.all_to_all(packed, 'row', 0, 0, tiled=True)  25.4 us
    all_to_all x1, blocking collectives, shards(): gathered = lax.all_to_all(picked, 'row', 0, 0, tiled=True)  19.2 us
    unnamed x8, local copies, waits for them, and re-layouts  2.95 us
    pallas_call x1, Pallas kernels, shards(): pl.pallas_call(lambda *refs: pick_kernel(tiles_here, blocks_per_col, *ref...  2.43 us
    pallas_call x1, Pallas kernels, shards(): pl.pallas_call(lambda *refs: pack_kernel(tiles_here, *refs), out_shape=(s...  1.94 us

profile of v1, /device:TPU:56, one launch (start us, length us, event | category | flops | bytes accessed | tf_op | source)
XLA Modules:
  0.0 78.9 jit_solution(3509260693654962364)
XLA Ops:
  1.3 1.9 %pack.1 = (f32[32,2,896]{2,1,0:T(2,128)}, s32[1]{0:T(128)}) custom-call(s32[192]{0:T(256)} %refs_0_.3, s32[1]{0:T(128)S(6)} %copy.6.refs_1_, f32[64,768]{1,0:T(8,128)} %bitcast.2, f32[6,128]{1,0:T(8,128)} %bitcast.4), custom_call_target="tpu_custom_call" | custom-call | tf_op jit(solution)/shard_map/pack/pallas_call | solution.py:216
  3.2 25.4 %all_to_all.10.refs_1_ = f32[32,2,896]{2,1,0:T(2,128)} all-to-all(f32[32,2,896]{2,1,0:T(2,128)} %get-tuple-element.7), channel_id=1, replica_groups=mesh['row'=32,'col'=16] {'row'}, dimensions={0} | all-to-all | bytes 458752 | tf_op jit(solution)/shard_map/all_to_all | solution.py:223
  28.6 2.4 %pick.1 = (f32[32,2,1664]{2,1,0:T(2,128)}, f32[1,128]{1,0:T(1,128)}) custom-call(s32[1]{0:T(128)} %get-tuple-element.6.refs_0_.refs_2_, f32[32,2,896]{2,1,0:T(2,128)} %all_to_all.10.refs_1_), custom_call_target="tpu_custom_call" | custom-call | tf_op jit(solution)/shard_map/pick/pallas_call | solution.py:224
  31.0 19.2 %all_to_all.11.refs_3_ = f32[32,2,1664]{2,1,0:T(2,128)S(1)} all-to-all(f32[32,2,1664]{2,1,0:T(2,128)} %get-tuple-element.8), channel_id=1, replica_groups=mesh['row'=32,'col'=16] {'row'}, dimensions={0} | all-to-all | bytes 851968 | tf_op jit(solution)/shard_map/all_to_all | solution.py:231
  50.2 0.0 copy-start
  50.2 0.9 %copy-done = f32[768,64]{0,1:T(8,128)S(1)} copy-done((f32[768,64]{0,1:T(8,128)S(1)}, f32[768,64]{0,1:T(8,128)}, u32[]{:S(2)}) %copy-start) | copy-done | bytes 196632
  51.2 0.0 copy-start.1
  51.2 0.7 copy-done.1
  51.8 0.0 copy-start.2
  51.8 0.7 copy-done.2
  52.5 0.0 copy-start.3
  52.5 0.7 copy-done.3
  53.2 25.7 %step.1 = (f32[768,128]{1,0:T(8,128)}, f32[768,1536]{1,0:T(8,128)}) custom-call(s32[192]{0:T(256)S(1)} %copy-done.2, s32[1]{0:T(128)S(6)} %copy.6.refs_1_, s32[1]{0:T(128)} %get-tuple-element.6.refs_0_.refs_2_, f32[32,2,1664]{2,1,0:T(2,128)S(1)} %all_to_all.11.refs_3_, f32[1,128]{1,0:T(1,128)S(1)} %copy-done.3, f32[64,768]{1,0:T(8,128)S(1)} %bitcast.3, ...), custom_call_target="tpu_custom_call" | custom-call | tf_op jit(solution)/shard_map/step/pallas_call | solution.py:233
Async XLA Ops:
  50.2 0.9 %copy-start = (f32[768,64]{0,1:T(8,128)S(1)}, f32[768,64]{0,1:T(8,128)}, u32[]{:S(2)}) copy-start(f32[768,64]{0,1:T(8,128)} %param.4) | copy-start | bytes 589828
  51.2 0.7 copy-start.1
  51.8 0.7 copy-start.2
  52.5 0.7 copy-start.3

commit v2 on v1

v2 whole, which is shorter than its diff:
```python
import jax
import jax.numpy as jnp
from jax import lax
from jax.experimental import pallas as pl
from jax.experimental.pallas import tpu as pltpu
from jax.sharding import PartitionSpec as P

TILE = 128
FEAT = 64
HIGHEST_MODE = lax.Precision.HIGHEST
F32 = jnp.float32
BF16 = jnp.bfloat16
VMEM = pltpu.VMEM
SMEM = pltpu.SMEM
CHUNK = 256
DEPTH = 3 * FEAT + 16
STEP_VMEM = 24 * 1024 * 1024


def vspec():
    return pl.BlockSpec(memory_space=VMEM)


def sspec():
    return pl.BlockSpec(memory_space=SMEM)


def pivot_slot_of(map_ref, panel_ref, tile_count):
    pivot = panel_ref[0]

    def step(s, slot):
        return jnp.where(map_ref[s] == pivot, s, slot)

    return lax.fori_loop(0, tile_count, step, jnp.int32(0), unroll=16)


def pack_kernel(tiles_here, map_ref, panel_ref, feat_ref, noise_ref, out_ref, slot_ref):
    slot = pivot_slot_of(map_ref, panel_ref, map_ref.shape[0])
    slot_ref[0] = slot
    slot_ref[1] = panel_ref[0]
    local = jnp.clip(slot - lax.axis_index("row") * tiles_here, 0, tiles_here - 1)
    rows = feat_ref.shape[1]
    extra = jnp.broadcast_to(noise_ref[pl.ds(local, 1), :], (2, TILE))
    for r in range(out_ref.shape[0]):
        out_ref[r, :, :rows] = feat_ref[2 * r : 2 * r + 2, :]
        out_ref[r, :, rows:] = extra


def pick_kernel(tiles_here, blocks_per_col, slot_ref, got_ref, out_ref, noise_ref):
    slot = slot_ref[0]
    rows = tiles_here * TILE
    first = lax.axis_index("col") * blocks_per_col
    owner = slot // tiles_here
    offset = pl.multiple_of((slot - owner * tiles_here) * TILE, TILE)
    noise_ref[...] = got_ref[owner, 0:1, rows:]
    parts = [got_ref[first + m, :, :rows] for m in range(blocks_per_col)]
    parts.append(got_ref[owner, :, pl.ds(offset, TILE)])
    for r in range(out_ref.shape[0]):
        at = 0
        for part in parts:
            out_ref[r, :, at : at + part.shape[1]] = part
            at += part.shape[1]


def split2(x):
    hi = x.astype(BF16).astype(F32)
    return hi, x - hi


def split3(x):
    a = x.astype(BF16).astype(F32)
    b = (x - a).astype(BF16).astype(F32)
    return a, b, x - a - b


def tail(norm, mine_first):
    n = norm.shape[1]
    at = lax.broadcasted_iota(jnp.int32, (16, n), 0)
    a, b, c = (jnp.broadcast_to(-v, (16, n)) for v in split3(norm))
    base = 0 if mine_first else 3
    out = jnp.where((at >= 3 - base) & (at < 6 - base), 1.0, 0.0)
    for i, v in enumerate((a, b, c)):
        out = jnp.where(at == base + i, v, out)
    return out


def left_side(feat_t):
    norm = jnp.sum(feat_t * feat_t, axis=0, keepdims=True) * (1.0 / FEAT)
    hi, lo = split2(feat_t)
    return jnp.concatenate([hi, hi, lo, tail(norm, True)], axis=0)


def right_side(feat_t):
    norm = jnp.sum(feat_t * feat_t, axis=0, keepdims=True) * (1.0 / FEAT)
    hi, lo = split2(feat_t * (2.0 / FEAT))
    return jnp.concatenate([hi, lo, hi, tail(norm, False)], axis=0).astype(BF16)


def inverse_factor(gram, inv_ref, tasks):
    count = TILE // 8
    full = (8, TILE)
    steps, done = 8 * count, 0
    w = [gram[8 * t : 8 * t + 8, :] for t in range(count)]
    lane = lax.broadcasted_iota(jnp.int32, full, 1)
    sub = lax.broadcasted_iota(jnp.int32, full, 0)
    for b in range(count):
        lo = 8 * b
        inside = (lane >= lo) & (lane < lo + 8)
        c = [jnp.broadcast_to(w[b][:, lo + k : lo + k + 1], full) for k in range(8)]
        r = jnp.where(inside, jnp.where(lane - lo == sub, 1.0, 0.0), w[b])
        out = jnp.zeros(full, F32)
        for s in range(8):
            mine = sub == s
            row = jnp.broadcast_to(r[s : s + 1, :], full)
            piv = jnp.broadcast_to(c[s][s : s + 1, :], full)
            inv = 1.0 / piv
            m = c[s] * inv
            for k in range(s + 1, 8):
                ck = jnp.broadcast_to(c[k][s : s + 1, :], full)
                c[k] = jnp.where(mine, ck * inv, c[k] - m * ck)
            out = jnp.where(mine, row * lax.rsqrt(piv), out)
            r = jnp.where(mine, row * inv, r - m * row)
            upto = len(tasks) * (lo + s + 1) // steps
            for task in tasks[done:upto]:
                task()
            done = upto
        inv_ref[lo : lo + 8, :] = jnp.where(lane < lo + 8, out, 0.0)
        y = [jnp.broadcast_to(r[k : k + 1, :], full) for k in range(8)]
        for t in range(b + 1, count):
            g = [jnp.broadcast_to(w[t][:, lo + k : lo + k + 1], full) * y[k] for k in range(8)]
            total = ((g[0] + g[1]) + (g[2] + g[3])) + ((g[4] + g[5]) + (g[6] + g[7]))
            w[t] = jnp.where(inside, 0.0, w[t]) - total


def dot(a, b, precision=None):
    return jnp.dot(a, b, precision=precision, preferred_element_type=F32)


def left_kernel(feat_ref, left_ref):
    for i in range(feat_ref.shape[1] // TILE):
        here = slice(i * TILE, (i + 1) * TILE)
        left_ref[here, :] = left_side(feat_ref[:, here]).T.astype(BF16)


def step_kernel(
    tiles_here,
    got_ref,
    map_hbm,
    slot_hbm,
    pivot_noise_hbm,
    noise_hbm,
    left_hbm,
    panel_hbm,
    trailing_hbm,
    map_ref,
    slot_ref,
    pivot_noise_ref,
    noise_ref,
    left_ref,
    in_sems,
    all_t,
    inv_ref,
    right_ref,
    row_kern_ref,
    col_kern_ref,
    col_panel_ref,
    row_panel_ref,
    panel_ref,
    out_ref,
    out_sems,
):
    cols = out_ref.shape[1]
    tiles_across = cols // TILE
    loads = [
        pltpu.make_async_copy(src, dst, in_sems.at[n])
        for n, (src, dst) in enumerate(
            (
                (pivot_noise_hbm, pivot_noise_ref),
                (left_hbm, left_ref),
                (map_hbm, map_ref),
                (slot_hbm, slot_ref),
                (noise_hbm, noise_ref),
            )
        )
    ]
    for load in loads:
        load.start()
    first_row_slot = lax.axis_index("row") * tiles_here
    first_col_slot = lax.axis_index("col") * tiles_across
    at_row = lax.broadcasted_iota(jnp.int32, (TILE, TILE), 0)
    at_col = lax.broadcasted_iota(jnp.int32, (TILE, TILE), 1)
    diagonal = at_row == at_col
    for r in range(got_ref.shape[0]):
        all_t[2 * r : 2 * r + 2, :] = got_ref[r]
    pivot_t = all_t[:, cols:]
    pivot_norm = jnp.sum(pivot_t * pivot_t, axis=0, keepdims=True)
    pivot_rows = pivot_t.T
    pivot_norm_col = jnp.sum(pivot_rows * pivot_rows, axis=1, keepdims=True)
    inner = dot(pivot_rows, pivot_t, HIGHEST_MODE)
    gram = jnp.exp((2.0 * inner - pivot_norm_col - pivot_norm) * (1.0 / FEAT))
    pivot_left = left_side(pivot_t).T.astype(BF16)
    pivot_right = right_side(pivot_t)
    for load in loads:
        load.wait()
    slot = slot_ref[0]
    pivot = slot_ref[1]
    pivot_noise = jnp.where(diagonal, pivot_noise_ref[...], 0.0)

    def right_task(j):
        here = slice(j * TILE, (j + 1) * TILE)
        right_ref[:, here] = right_side(all_t[:, here])

    def col_task(j):
        here = slice(j * TILE, (j + 1) * TILE)
        kern = jnp.exp(dot(pivot_left, right_ref[:, here]))
        hi, lo = split2(kern + jnp.where(first_col_slot + j == slot, pivot_noise, 0.0))
        col_kern_ref[:, here] = jnp.concatenate([hi, lo, hi], axis=0).astype(BF16)

    def row_task(i):
        here = slice(i * TILE, (i + 1) * TILE)
        kern = jnp.exp(dot(left_ref[here, :], pivot_right))
        hi, lo = split2(kern + jnp.where(first_row_slot + i == slot, pivot_noise, 0.0))
        row_kern_ref[here, :] = jnp.concatenate([hi, hi, lo], axis=1).astype(BF16)

    def kern_task(i, n):
        here, part = slice(i * TILE, (i + 1) * TILE), slice(n * CHUNK, (n + 1) * CHUNK)
        out_ref[here, part] = jnp.exp(dot(left_ref[here, :], right_ref[:, part]))

    def later(fn, *args):
        return lambda: fn(*args)

    tasks = [later(right_task, j) for j in range(tiles_across)]
    tasks += [later(col_task, j) for j in range(tiles_across)]
    tasks += [later(row_task, i) for i in range(tiles_here)]
    tasks += [later(kern_task, i, n) for n in range(cols // CHUNK) for i in range(tiles_here)]
    inverse_factor(gram + pivot_noise, inv_ref, tasks)

    hi, lo = split2(inv_ref[...])
    inv_left = jnp.concatenate([hi, hi, lo], axis=1).astype(BF16)
    inv_right = jnp.concatenate([hi, lo, hi], axis=1).astype(BF16)
    for i in range(tiles_here):
        here = slice(i * TILE, (i + 1) * TILE)
        factor = lax.dot_general(
            row_kern_ref[here, :],
            inv_right,
            (((1,), (1,)), ((), ())),
            preferred_element_type=F32,
        )
        factor = jnp.where(map_ref[first_row_slot + i] >= pivot, factor, 0.0)
        panel_ref[here, :] = factor
        hi, lo = split2(factor)
        row_panel_ref[here, :] = jnp.concatenate([hi, hi, lo], axis=1).astype(BF16)
    panel_copy = pltpu.make_async_copy(panel_ref, panel_hbm, out_sems.at[0])
    panel_copy.start()
    for n in range(cols // CHUNK):
        part = slice(n * CHUNK, (n + 1) * CHUNK)
        hi, lo = split2(dot(inv_left, col_kern_ref[:, part]))
        col_panel_ref[:, part] = jnp.concatenate([hi, lo, hi], axis=0).astype(BF16)

    ahead = first_row_slot - first_col_slot

    @pl.when((ahead >= 0) & (ahead < tiles_across))
    def _():
        for i in range(tiles_here):
            here = slice(i * TILE, (i + 1) * TILE)
            part = pl.ds(pl.multiple_of((ahead + i) * TILE, TILE), TILE)
            out_ref[here, part] += jnp.where(diagonal, noise_ref[i : i + 1, :], 0.0)

    copies = [panel_copy]
    per_chunk = CHUNK // TILE
    for n in range(cols // CHUNK):
        across = slice(n * CHUNK, (n + 1) * CHUNK)
        for i in range(tiles_here):
            here = slice(i * TILE, (i + 1) * TILE)
            taken = dot(row_panel_ref[here, :], col_panel_ref[:, across])
            row_tile = map_ref[first_row_slot + i]
            for h in range(per_chunk):
                col_tile = map_ref[first_col_slot + n * per_chunk + h]
                live = (row_tile >= col_tile) & (col_tile > pivot)
                part = slice(n * CHUNK + h * TILE, n * CHUNK + (h + 1) * TILE)
                value = out_ref[here, part] - taken[:, h * TILE : (h + 1) * TILE]
                out_ref[here, part] = jnp.where(live, value, 0.0)
        copy = pltpu.make_async_copy(
            out_ref.at[:, across], trailing_hbm.at[:, across], out_sems.at[1 + n]
        )
        copy.start()
        copies.append(copy)
    for copy in copies:
        copy.wait()


def left_call(tiles_here, feat_t):
    rows = tiles_here * TILE
    return pl.pallas_call(
        left_kernel,
        out_shape=jax.ShapeDtypeStruct((rows, DEPTH), BF16),
        in_specs=[vspec()],
        out_specs=vspec(),
        cost_estimate=pl.CostEstimate(flops=10**9, bytes_accessed=5 * 10**6, transcendentals=0),
        name="left",
    )(feat_t)


def step_call(tiles_here, cols, *args):
    rows = tiles_here * TILE
    hspec = pl.BlockSpec(memory_space=pltpu.HBM)
    shape = jax.ShapeDtypeStruct
    return pl.pallas_call(
        lambda *refs: step_kernel(tiles_here, *refs),
        out_shape=(shape((rows, TILE), F32), shape((rows, cols), F32)),
        in_specs=[vspec()] + [hspec] * 5,
        out_specs=(hspec, hspec),
        scratch_shapes=[
            SMEM(args[1].shape, jnp.int32),
            SMEM(args[2].shape, jnp.int32),
            VMEM((1, TILE), F32),
            VMEM((tiles_here, TILE), F32),
            VMEM((rows, DEPTH), BF16),
            pltpu.SemaphoreType.DMA((5,)),
            VMEM((FEAT, cols + TILE), F32),
            VMEM((TILE, TILE), F32),
            VMEM((DEPTH, cols), BF16),
            VMEM((rows, 3 * TILE), BF16),
            VMEM((3 * TILE, cols), BF16),
            VMEM((3 * TILE, cols), BF16),
            VMEM((rows, 3 * TILE), BF16),
            VMEM((rows, TILE), F32),
            VMEM((rows, cols), F32),
            pltpu.SemaphoreType.DMA((1 + cols // CHUNK,)),
        ],
        compiler_params=pltpu.CompilerParams(vmem_limit_bytes=STEP_VMEM),
        name="step",
    )(*args)


def shards(features, noise, tile_map, panel_tile):
    rows_here = features.shape[0]
    tiles_here = rows_here // TILE
    members = lax.axis_size("row")
    blocks_per_col = members // lax.axis_size("col")
    cols = rows_here * blocks_per_col
    feat_t = features.T
    noise_2d = noise.reshape(tiles_here, TILE)
    shape = jax.ShapeDtypeStruct
    packed, slot = pl.pallas_call(
        lambda *refs: pack_kernel(tiles_here, *refs),
        out_shape=(shape((members, 2, rows_here + TILE), F32), shape((2,), jnp.int32)),
        in_specs=[sspec(), sspec(), vspec(), vspec()],
        out_specs=(vspec(), sspec()),
        name="pack",
    )(tile_map, panel_tile, feat_t, noise_2d)
    got = lax.all_to_all(packed, "row", 0, 0, tiled=True)
    picked, pivot_noise = pl.pallas_call(
        lambda *refs: pick_kernel(tiles_here, blocks_per_col, *refs),
        out_shape=(shape((members, 2, cols + TILE), F32), shape((1, TILE), F32)),
        in_specs=[sspec(), vspec()],
        out_specs=(vspec(), vspec()),
        name="pick",
    )(slot, got)
    gathered = lax.all_to_all(picked, "row", 0, 0, tiled=True)
    left = left_call(tiles_here, feat_t)
    held = [
        pltpu.with_memory_space_constraint(x, pltpu.HBM)
        for x in (tile_map, slot, pivot_noise, noise_2d, left)
    ]
    return step_call(tiles_here, cols, gathered, *held)


def solution(mesh):
    in_specs = (P("row", None), P("row"), P(), P())
    out_specs = (P("row", None), P("row", "col"))
    return jax.shard_map(shards, mesh=mesh, in_specs=in_specs, out_specs=out_specs, check_vma=False)
```

time: 79.3 us -> 59.3 us (0.75)
  blocking collectives: 44.6 us -> 25.4 us
  Pallas kernels: 30.1 us -> 15 us
  waiting for transfers between devices: 0 us -> 13.3 us
  starting transfers between devices: 0 us -> 3.97 us
  local copies, waits for them, and re-layouts: 2.95 us -> 0 us
    all_to_all x1 -> x0, blocking collectives: 19.2 us -> none  [shards(): gathered = lax.all_to_all(picked, 'row', 0, 0, tiled=True)]
    pallas_call x1 -> x2, Pallas kernels: 25.7 us -> 11.3 us  [the longest x1 9.39 us: step_call(): pl.pallas_call(lambda *refs: step_kernel(tiles_here, *refs), out_shape=(s...]
    all_to_all x0 -> x1, waiting for transfers between devices: none -> 13.3 us  [shards(): gathered = lax.all_to_all(picked, 'row', 0, 0, tiled=True)]
    all_to_all x0 -> x1, starting transfers between devices: none -> 3.97 us  [shards(): gathered = lax.all_to_all(picked, 'row', 0, 0, tiled=True)]
    unnamed x8 -> x0, local copies, waits for them, and re-layouts: 2.95 us -> none
  transfers between devices with their start and end apart: 0 -> 1, of which waited for: 0 -> 1; matrix products, arithmetic and copies ran while one was open for 0% -> 0% of each run, Pallas kernels for 0% -> 3%
where the time goes in v2:
time: 59.3 us; the launch traced here: 59 us
  blocking collectives  25.4 us (43%)
  Pallas kernels  15 us (25%)
  waiting for transfers between devices  13.3 us (22%)
  starting transfers between devices  3.97 us (7%)
  between operations  1.29 us (2%)
    all_to_all x1, blocking collectives, shards(): got = lax.all_to_all(packed, 'row', 0, 0, tiled=True)  25.4 us
    all_to_all x1, waiting for transfers between devices, shards(): gathered = lax.all_to_all(picked, 'row', 0, 0, tiled=True)  13.3 us
    pallas_call x1, Pallas kernels, step_call(): pl.pallas_call(lambda *refs: step_kernel(tiles_here, *refs), out_shape=(s...  9.39 us
    all_to_all x1, starting transfers between devices, shards(): gathered = lax.all_to_all(picked, 'row', 0, 0, tiled=True)  3.97 us
    pallas_call x1, Pallas kernels, shards(): pl.pallas_call(lambda *refs: pack_kernel(tiles_here, *refs), out_shape=(s...  1.95 us
    pallas_call x1, Pallas kernels, left_call(): pl.pallas_call(left_kernel, out_shape=jax.ShapeDtypeStruct((rows, DEPTH),...  1.87 us
    pallas_call x1, Pallas kernels, shards(): pl.pallas_call(lambda *refs: pick_kernel(tiles_here, blocks_per_col, *ref...  1.76 us
  transfers between devices with their start and end apart: 1, of which 1 were waited for; matrix products, arithmetic and copies ran while one was open for 0% of the time, Pallas kernels for 3%

profile of v2, /device:TPU:56, one launch (start us, length us, event | category | flops | bytes accessed | tf_op | source)
XLA Modules:
  0.0 59.0 jit_solution(3269112960661828812)
XLA Ops:
  1.3 1.9 %pack.1 = (f32[32,2,896]{2,1,0:T(2,128)}, s32[2]{0:T(128)}) custom-call(s32[192]{0:T(256)} %refs_1_.2, s32[1]{0:T(128)S(6)} %copy.6.refs_1_, f32[64,768]{1,0:T(8,128)} %bitcast.2, f32[6,128]{1,0:T(8,128)} %bitcast.4), custom_call_target="tpu_custom_call" | custom-call | tf_op jit(solution)/shard_map/pack/pallas_call | solution.py:345
  3.2 25.4 %all_to_all.10.refs_1_ = f32[32,2,896]{2,1,0:T(2,128)} all-to-all(f32[32,2,896]{2,1,0:T(2,128)} %get-tuple-element.7), channel_id=1, replica_groups=mesh['row'=32,'col'=16] {'row'}, dimensions={0} | all-to-all | bytes 458752 | tf_op jit(solution)/shard_map/all_to_all | solution.py:352
  28.6 1.8 %pick.1 = (f32[32,2,1664]{2,1,0:T(2,128)}, f32[1,128]{1,0:T(1,128)}) custom-call(s32[2]{0:T(128)} %get-tuple-element.6.refs_0_.refs_2_, f32[32,2,896]{2,1,0:T(2,128)} %all_to_all.10.refs_1_), custom_call_target="tpu_custom_call" | custom-call | tf_op jit(solution)/shard_map/pick/pallas_call | solution.py:353
  30.4 4.0 %all-to-all-start.1 = ((f32[32,2,1664]{2,1,0:T(2,128)}), f32[32,2,1664]{2,1,0:T(2,128)S(1)}, u32[]{:S(2)}, u32[]{:S(2)}) async-start(f32[32,2,1664]{2,1,0:T(2,128)} %get-tuple-element.8), calls=%async_computation.1 | async-start | bytes 851968 | tf_op jit(solution)/shard_map/all_to_all | solution.py:360
  34.4 1.9 %left.1.refs_5_ = bf16[768,208]{1,0:T(8,128)(2,1)} custom-call(f32[64,768]{1,0:T(8,128)} %bitcast.3), custom_call_target="tpu_custom_call" | custom-call | flops 1000000000 | bytes 5000000 | tf_op jit(solution)/shard_map/left/pallas_call | solution.py:294
  36.2 13.3 %all-to-all-done.1.refs_0_ = f32[32,2,1664]{2,1,0:T(2,128)S(1)} async-done(((f32[32,2,1664]{2,1,0:T(2,128)}), f32[32,2,1664]{2,1,0:T(2,128)S(1)}, u32[]{:S(2)}, u32[]{:S(2)}) %all-to-all-start.1) | async-done | bytes 426016 | tf_op jit(solution)/shard_map/all_to_all | solution.py:360
  49.6 9.4 %step.1 = (f32[768,128]{1,0:T(8,128)}, f32[768,1536]{1,0:T(8,128)}) custom-call(f32[32,2,1664]{2,1,0:T(2,128)S(1)} %all-to-all-done.1.refs_0_, s32[192]{0:T(256)} %refs_1_.2, s32[2]{0:T(128)} %get-tuple-element.6.refs_0_.refs_2_, f32[1,128]{1,0:T(1,128)} %get-tuple-element.9.refs_3_, f32[6,128]{1,0:T(8,128)} %bitcast.5, bf16[768,208]{1,0:T(8,128)(2,1)} %left.1.refs_5_), custom_call_target="tpu_custom_call" | custom-call | tf_op jit(solution)/shard_map/step/pallas_call | solution.py:308
Async XLA Ops:
  30.4 19.2 %all-to-all-start.1 = ((f32[32,2,1664]{2,1,0:T(2,128)}), f32[32,2,1664]{2,1,0:T(2,128)S(1)}, u32[]{:S(2)}, u32[]{:S(2)}) async-start(f32[32,2,1664]{2,1,0:T(2,128)} %get-tuple-element.8), calls=%async_computation.1 | async-start | bytes 851968 | tf_op jit(solution)/shard_map/all_to_all | solution.py:360

commit v3 on v2

--- a/solution.py
+++ b/solution.py
@@ -31,7 +31,7 @@
     def step(s, slot):
         return jnp.where(map_ref[s] == pivot, s, slot)
 
-    return lax.fori_loop(0, tile_count, step, jnp.int32(0), unroll=16)
+    return lax.fori_loop(0, tile_count, step, jnp.int32(0), unroll=True)
 
 
 def pack_kernel(tiles_here, map_ref, panel_ref, feat_ref, noise_ref, out_ref, slot_ref):
@@ -52,7 +52,7 @@
     first = lax.axis_index("col") * blocks_per_col
     owner = slot // tiles_here
     offset = pl.multiple_of((slot - owner * tiles_here) * TILE, TILE)
-    noise_ref[...] = got_ref[owner, 0:1, rows:]
+    noise_ref[...] = got_ref[owner, :, rows:]
     parts = [got_ref[first + m, :, :rows] for m in range(blocks_per_col)]
     parts.append(got_ref[owner, :, pl.ds(offset, TILE)])
     for r in range(out_ref.shape[0]):
@@ -99,65 +99,74 @@
 def inverse_factor(gram, inv_ref, tasks):
     count = TILE // 8
     full = (8, TILE)
-    steps, done = 8 * count, 0
+    steps, done = 4 * count, 0
     w = [gram[8 * t : 8 * t + 8, :] for t in range(count)]
     lane = lax.broadcasted_iota(jnp.int32, full, 1)
     sub = lax.broadcasted_iota(jnp.int32, full, 0)
+
+    def across(v, k):
+        return jnp.broadcast_to(v[:, k : k + 1], full)
+
+    def down(v, k):
+        return jnp.broadcast_to(v[k : k + 1, :], full)
+
     for b in range(count):
         lo = 8 * b
         inside = (lane >= lo) & (lane < lo + 8)
-        c = [jnp.broadcast_to(w[b][:, lo + k : lo + k + 1], full) for k in range(8)]
+        c = [across(w[b], lo + k) for k in range(8)]
         r = jnp.where(inside, jnp.where(lane - lo == sub, 1.0, 0.0), w[b])
         out = jnp.zeros(full, F32)
-        for s in range(8):
-            mine = sub == s
-            row = jnp.broadcast_to(r[s : s + 1, :], full)
-            piv = jnp.broadcast_to(c[s][s : s + 1, :], full)
-            inv = 1.0 / piv
-            m = c[s] * inv
-            for k in range(s + 1, 8):
-                ck = jnp.broadcast_to(c[k][s : s + 1, :], full)
-                c[k] = jnp.where(mine, ck * inv, c[k] - m * ck)
-            out = jnp.where(mine, row * lax.rsqrt(piv), out)
-            r = jnp.where(mine, row * inv, r - m * row)
-            upto = len(tasks) * (lo + s + 1) // steps
+        for s in range(0, 8, 2):
+            first, second = sub == s, sub == s + 1
+            row0, row1 = down(r, s), down(r, s + 1)
+            p, q, d = down(c[s], s), down(c[s], s + 1), down(c[s + 1], s + 1)
+            inv_p = 1.0 / p
+            det = p * d - q * q
+            inv_det = 1.0 / det
+            i00, i01, i11 = d * inv_det, -q * inv_det, p * inv_det
+            below = row1 - (q * inv_p) * row0
+            out = jnp.where(first, row0 * lax.rsqrt(p), out)
+            out = jnp.where(second, below * lax.rsqrt(det * inv_p), out)
+            u = jnp.where(second, -i01, c[s] * i00 + c[s + 1] * i01)
+            u = jnp.where(first, 1.0 - i00, u)
+            v = jnp.where(second, 1.0 - i11, c[s] * i01 + c[s + 1] * i11)
+            v = jnp.where(first, -i01, v)
+            for k in range(s + 2, 8):
+                c[k] = c[k] - (u * down(c[k], s) + v * down(c[k], s + 1))
+            r = r - (u * row0 + v * row1)
+            upto = len(tasks) * (4 * b + s // 2 + 1) // steps
             for task in tasks[done:upto]:
                 task()
             done = upto
         inv_ref[lo : lo + 8, :] = jnp.where(lane < lo + 8, out, 0.0)
-        y = [jnp.broadcast_to(r[k : k + 1, :], full) for k in range(8)]
+        y = [down(r, k) for k in range(8)]
         for t in range(b + 1, count):
-            g = [jnp.broadcast_to(w[t][:, lo + k : lo + k + 1], full) * y[k] for k in range(8)]
+            g = [across(w[t], lo + k) * y[k] for k in range(8)]
             total = ((g[0] + g[1]) + (g[2] + g[3])) + ((g[4] + g[5]) + (g[6] + g[7]))
             w[t] = jnp.where(inside, 0.0, w[t]) - total
 
 
 def dot(a, b, precision=None):
     return jnp.dot(a, b, precision=precision, preferred_element_type=F32)
-
-
-def left_kernel(feat_ref, left_ref):
-    for i in range(feat_ref.shape[1] // TILE):
-        here = slice(i * TILE, (i + 1) * TILE)
-        left_ref[here, :] = left_side(feat_ref[:, here]).T.astype(BF16)
 
 
 def step_kernel(
     tiles_here,
     got_ref,
+    pivot_noise_ref,
     map_hbm,
     slot_hbm,
-    pivot_noise_hbm,
     noise_hbm,
-    left_hbm,
+    feat_hbm,
     panel_hbm,
     trailing_hbm,
     map_ref,
     slot_ref,
-    pivot_noise_ref,
     noise_ref,
+    feat_ref,
     left_ref,
     in_sems,
+    pivot_t_ref,
     all_t,
     inv_ref,
     right_ref,
@@ -171,54 +180,62 @@
 ):
     cols = out_ref.shape[1]
     tiles_across = cols // TILE
+    meta_load = pltpu.make_async_copy(slot_hbm, slot_ref, in_sems.at[0])
+    meta_load.start()
     loads = [
-        pltpu.make_async_copy(src, dst, in_sems.at[n])
+        pltpu.make_async_copy(src, dst, in_sems.at[1 + n])
         for n, (src, dst) in enumerate(
-            (
-                (pivot_noise_hbm, pivot_noise_ref),
-                (left_hbm, left_ref),
-                (map_hbm, map_ref),
-                (slot_hbm, slot_ref),
-                (noise_hbm, noise_ref),
-            )
+            ((feat_hbm, feat_ref), (map_hbm, map_ref), (noise_hbm, noise_ref))
         )
     ]
     for load in loads:
         load.start()
+    for r in range(got_ref.shape[0]):
+        pivot_t_ref[2 * r : 2 * r + 2, :] = got_ref[r, :, cols:]
     first_row_slot = lax.axis_index("row") * tiles_here
     first_col_slot = lax.axis_index("col") * tiles_across
     at_row = lax.broadcasted_iota(jnp.int32, (TILE, TILE), 0)
     at_col = lax.broadcasted_iota(jnp.int32, (TILE, TILE), 1)
     diagonal = at_row == at_col
-    for r in range(got_ref.shape[0]):
-        all_t[2 * r : 2 * r + 2, :] = got_ref[r]
-    pivot_t = all_t[:, cols:]
+    pivot_t = pivot_t_ref[...]
     pivot_norm = jnp.sum(pivot_t * pivot_t, axis=0, keepdims=True)
     pivot_rows = pivot_t.T
     pivot_norm_col = jnp.sum(pivot_rows * pivot_rows, axis=1, keepdims=True)
     inner = dot(pivot_rows, pivot_t, HIGHEST_MODE)
     gram = jnp.exp((2.0 * inner - pivot_norm_col - pivot_norm) * (1.0 / FEAT))
-    pivot_left = left_side(pivot_t).T.astype(BF16)
-    pivot_right = right_side(pivot_t)
-    for load in loads:
-        load.wait()
+    meta_load.wait()
     slot = slot_ref[0]
     pivot = slot_ref[1]
-    pivot_noise = jnp.where(diagonal, pivot_noise_ref[...], 0.0)
+    pivot_noise = jnp.where(diagonal, pivot_noise_ref[0:1, :], 0.0)
+    held = {}
+
+    def pivot_task():
+        held["left"] = left_side(pivot_t).T.astype(BF16)
+        held["right"] = right_side(pivot_t)
+
+    def wait_task():
+        for load in loads:
+            load.wait()
+
+    def left_task(i):
+        here = slice(i * TILE, (i + 1) * TILE)
+        left_ref[here, :] = left_side(feat_ref[:, here]).T.astype(BF16)
 
     def right_task(j):
         here = slice(j * TILE, (j + 1) * TILE)
+        for r in range(got_ref.shape[0]):
+            all_t[2 * r : 2 * r + 2, here] = got_ref[r, :, here]
         right_ref[:, here] = right_side(all_t[:, here])
 
     def col_task(j):
         here = slice(j * TILE, (j + 1) * TILE)
-        kern = jnp.exp(dot(pivot_left, right_ref[:, here]))
+        kern = jnp.exp(dot(held["left"], right_ref[:, here]))
         hi, lo = split2(kern + jnp.where(first_col_slot + j == slot, pivot_noise, 0.0))
         col_kern_ref[:, here] = jnp.concatenate([hi, lo, hi], axis=0).astype(BF16)
 
     def row_task(i):
         here = slice(i * TILE, (i + 1) * TILE)
-        kern = jnp.exp(dot(left_ref[here, :], pivot_right))
+        kern = jnp.exp(dot(left_ref[here, :], held["right"]))
         hi, lo = split2(kern + jnp.where(first_row_slot + i == slot, pivot_noise, 0.0))
         row_kern_ref[here, :] = jnp.concatenate([hi, hi, lo], axis=1).astype(BF16)
 
@@ -229,8 +246,9 @@
     def later(fn, *args):
         return lambda: fn(*args)
 
-    tasks = [later(right_task, j) for j in range(tiles_across)]
+    tasks = [later(right_task, j) for j in range(tiles_across)] + [pivot_task]
     tasks += [later(col_task, j) for j in range(tiles_across)]
+    tasks += [wait_task] + [later(left_task, i) for i in range(tiles_here)]
     tasks += [later(row_task, i) for i in range(tiles_here)]
     tasks += [later(kern_task, i, n) for n in range(cols // CHUNK) for i in range(tiles_here)]
     inverse_factor(gram + pivot_noise, inv_ref, tasks)
@@ -289,18 +307,6 @@
         copy.wait()
 
 
-def left_call(tiles_here, feat_t):
-    rows = tiles_here * TILE
-    return pl.pallas_call(
-        left_kernel,
-        out_shape=jax.ShapeDtypeStruct((rows, DEPTH), BF16),
-        in_specs=[vspec()],
-        out_specs=vspec(),
-        cost_estimate=pl.CostEstimate(flops=10**9, bytes_accessed=5 * 10**6, transcendentals=0),
-        name="left",
-    )(feat_t)
-
-
 def step_call(tiles_here, cols, *args):
     rows = tiles_here * TILE
     hspec = pl.BlockSpec(memory_space=pltpu.HBM)
@@ -308,16 +314,17 @@
     return pl.pallas_call(
         lambda *refs: step_kernel(tiles_here, *refs),
         out_shape=(shape((rows, TILE), F32), shape((rows, cols), F32)),
-        in_specs=[vspec()] + [hspec] * 5,
+        in_specs=[vspec(), vspec()] + [hspec] * 4,
         out_specs=(hspec, hspec),
         scratch_shapes=[
-            SMEM(args[1].shape, jnp.int32),
             SMEM(args[2].shape, jnp.int32),
-            VMEM((1, TILE), F32),
+            SMEM(args[3].shape, jnp.int32),
             VMEM((tiles_here, TILE), F32),
+            VMEM((FEAT, rows), F32),
             VMEM((rows, DEPTH), BF16),
-            pltpu.SemaphoreType.DMA((5,)),
-            VMEM((FEAT, cols + TILE), F32),
+            pltpu.SemaphoreType.DMA((4,)),
+            VMEM((FEAT, TILE), F32),
+            VMEM((FEAT, cols), F32),
             VMEM((TILE, TILE), F32),
             VMEM((DEPTH, cols), BF16),
             VMEM((rows, 3 * TILE), BF16),
@@ -344,26 +351,26 @@
     shape = jax.ShapeDtypeStruct
     packed, slot = pl.pallas_call(
         lambda *refs: pack_kernel(tiles_here, *refs),
-        out_shape=(shape((members, 2, rows_here + TILE), F32), shape((2,), jnp.int32)),
+        out_shape=(VMEM((members, 2, rows_here + TILE), F32), shape((2,), jnp.int32)),
         in_specs=[sspec(), sspec(), vspec(), vspec()],
         out_specs=(vspec(), sspec()),
         name="pack",
     )(tile_map, panel_tile, feat_t, noise_2d)
     got = lax.all_to_all(packed, "row", 0, 0, tiled=True)
+    got = pltpu.with_memory_space_constraint(got, VMEM)
     picked, pivot_noise = pl.pallas_call(
         lambda *refs: pick_kernel(tiles_here, blocks_per_col, *refs),
-        out_shape=(shape((members, 2, cols + TILE), F32), shape((1, TILE), F32)),
+        out_shape=(VMEM((members, 2, cols + TILE), F32), VMEM((2, TILE), F32)),
         in_specs=[sspec(), vspec()],
         out_specs=(vspec(), vspec()),
         name="pick",
     )(slot, got)
     gathered = lax.all_to_all(picked, "row", 0, 0, tiled=True)
-    left = left_call(tiles_here, feat_t)
     held = [
         pltpu.with_memory_space_constraint(x, pltpu.HBM)
-        for x in (tile_map, slot, pivot_noise, noise_2d, left)
+        for x in (tile_map, slot, noise_2d, feat_t)
     ]
-    return step_call(tiles_here, cols, gathered, *held)
+    return step_call(tiles_here, cols, gathered, pivot_noise, *held)
 
 
 def solution(mesh):

time: 59.3 us -> 56.7 us (0.956)
  blocking collectives: 25.4 us -> 44.1 us
  waiting for transfers between devices: 13.3 us -> 0 us
  starting transfers between devices: 3.97 us -> 0 us
  Pallas kernels: 15 us -> 11.1 us
    all_to_all x0 -> x1, blocking collectives: none -> 19 us  [shards(): gathered = lax.all_to_all(picked, 'row', 0, 0, tiled=True)]
    all_to_all x1 -> x0, waiting for transfers between devices: 13.3 us -> none  [shards(): gathered = lax.all_to_all(picked, 'row', 0, 0, tiled=True)]
    all_to_all x1 -> x0, starting transfers between devices: 3.97 us -> none  [shards(): gathered = lax.all_to_all(picked, 'row', 0, 0, tiled=True)]
    pallas_call x2 -> x1, Pallas kernels: 3.81 us -> 1.61 us  [shards(): pl.pallas_call(lambda *refs: pack_kernel(tiles_here, *refs), out_shape=(V...]
    pallas_call x1, Pallas kernels: 1.76 us -> 0.72 us  [shards(): pl.pallas_call(lambda *refs: pick_kernel(tiles_here, blocks_per_col, *ref...]
  transfers between devices with their start and end apart: 1 -> 0, of which waited for: 1 -> 0; matrix products, arithmetic and copies ran while one was open for 0% -> 0% of each run, Pallas kernels for 3% -> 0%
where the time goes in v3:
time: 56.7 us; the launch traced here: 56.5 us
  blocking collectives  44.1 us (78%)
  Pallas kernels  11.1 us (20%)
  between operations  1.29 us (2%)
    all_to_all x1, blocking collectives, shards(): got = lax.all_to_all(packed, 'row', 0, 0, tiled=True)  25.1 us
    all_to_all x1, blocking collectives, shards(): gathered = lax.all_to_all(picked, 'row', 0, 0, tiled=True)  19 us
    pallas_call x1, Pallas kernels, step_call(): pl.pallas_call(lambda *refs: step_kernel(tiles_here, *refs), out_shape=(s...  8.82 us
    pallas_call x1, Pallas kernels, shards(): pl.pallas_call(lambda *refs: pack_kernel(tiles_here, *refs), out_shape=(V...  1.61 us

profile of v3, /device:TPU:56, one launch (start us, length us, event | category | flops | bytes accessed | tf_op | source)
XLA Modules:
  0.0 56.5 jit_solution(17415841896692184336)
XLA Ops:
  1.3 1.6 %pack.1 = (f32[32,2,896]{2,1,0:T(2,128)S(1)}, s32[2]{0:T(128)}) custom-call(s32[192]{0:T(256)} %refs_2_.1, s32[1]{0:T(128)S(6)} %copy.6.refs_1_, f32[64,768]{1,0:T(8,128)} %bitcast.2, f32[6,128]{1,0:T(8,128)} %bitcast.4), custom_call_target="tpu_custom_call" | custom-call | tf_op jit(solution)/shard_map/pack/pallas_call | solution.py:352
  2.9 25.1 %all_to_all.10.refs_1_ = f32[32,2,896]{2,1,0:T(2,128)S(1)} all-to-all(f32[32,2,896]{2,1,0:T(2,128)S(1)} %get-tuple-element.7), channel_id=1, replica_groups=mesh['row'=32,'col'=16] {'row'}, dimensions={0} | all-to-all | bytes 458752 | tf_op jit(solution)/shard_map/all_to_all | solution.py:359
  28.0 0.7 %pick.1 = (f32[32,2,1664]{2,1,0:T(2,128)S(1)}, f32[2,128]{1,0:T(2,128)S(1)}) custom-call(s32[2]{0:T(128)} %get-tuple-element.6.refs_0_.refs_3_, f32[32,2,896]{2,1,0:T(2,128)S(1)} %all_to_all.10.refs_1_), custom_call_target="tpu_custom_call" | custom-call | tf_op jit(solution)/shard_map/pick/pallas_call | solution.py:361
  28.7 19.0 %all_to_all.11.refs_0_ = f32[32,2,1664]{2,1,0:T(2,128)S(1)} all-to-all(f32[32,2,1664]{2,1,0:T(2,128)S(1)} %get-tuple-element.8), channel_id=1, replica_groups=mesh['row'=32,'col'=16] {'row'}, dimensions={0} | all-to-all | bytes 851968 | tf_op jit(solution)/shard_map/all_to_all | solution.py:368
  47.7 8.8 %step.1 = (f32[768,128]{1,0:T(8,128)}, f32[768,1536]{1,0:T(8,128)}) custom-call(f32[32,2,1664]{2,1,0:T(2,128)S(1)} %all_to_all.11.refs_0_, f32[2,128]{1,0:T(2,128)S(1)} %get-tuple-element.9.refs_1_, s32[192]{0:T(256)} %refs_2_.1, s32[2]{0:T(128)} %get-tuple-element.6.refs_0_.refs_3_, f32[6,128]{1,0:T(8,128)} %bitcast.5, f32[64,768]{1,0:T(8,128)} %bitcast.3), custom_call_target="tpu_custom_call" | custom-call | tf_op jit(solution)/shard_map/step/pallas_call | solution.py:314

commit v4 on v3

--- a/solution.py
+++ b/solution.py
@@ -134,7 +134,7 @@
             for k in range(s + 2, 8):
                 c[k] = c[k] - (u * down(c[k], s) + v * down(c[k], s + 1))
             r = r - (u * row0 + v * row1)
-            upto = len(tasks) * (4 * b + s // 2 + 1) // steps
+            upto = max(0, len(tasks) * (4 * b + s // 2 + 1 - steps // 2) // (steps // 2))
             for task in tasks[done:upto]:
                 task()
             done = upto

time: 56.7 us -> 56 us (0.988)
  Pallas kernels: 11.1 us -> 10.5 us
    pallas_call x1, Pallas kernels: 8.82 us -> 8.15 us  [step_call(): pl.pallas_call(lambda *refs: step_kernel(tiles_here, *refs), out_shape=(s...]
where the time goes in v4:
time: 56 us; the launch traced here: 55.8 us
  blocking collectives  44.1 us (79%)
  Pallas kernels  10.5 us (19%)
  between operations  1.29 us (2%)
    all_to_all x1, blocking collectives, shards(): got = lax.all_to_all(packed, 'row', 0, 0, tiled=True)  25.1 us
    all_to_all x1, blocking collectives, shards(): gathered = lax.all_to_all(picked, 'row', 0, 0, tiled=True)  19 us
    pallas_call x1, Pallas kernels, step_call(): pl.pallas_call(lambda *refs: step_kernel(tiles_here, *refs), out_shape=(s...  8.15 us
    pallas_call x1, Pallas kernels, shards(): pl.pallas_call(lambda *refs: pack_kernel(tiles_here, *refs), out_shape=(V...  1.61 us

profile of v4, /device:TPU:56, one launch (start us, length us, event | category | flops | bytes accessed | tf_op | source)
XLA Modules:
  0.0 55.8 jit_solution(4446601453314690191)
XLA Ops:
  1.3 1.6 %pack.1 = (f32[32,2,896]{2,1,0:T(2,128)S(1)}, s32[2]{0:T(128)}) custom-call(s32[192]{0:T(256)} %refs_2_.1, s32[1]{0:T(128)S(6)} %copy.6.refs_1_, f32[64,768]{1,0:T(8,128)} %bitcast.2, f32[6,128]{1,0:T(8,128)} %bitcast.4), custom_call_target="tpu_custom_call" | custom-call | tf_op jit(solution)/shard_map/pack/pallas_call | solution.py:352
  2.9 25.1 %all_to_all.10.refs_1_ = f32[32,2,896]{2,1,0:T(2,128)S(1)} all-to-all(f32[32,2,896]{2,1,0:T(2,128)S(1)} %get-tuple-element.7), channel_id=1, replica_groups=mesh['row'=32,'col'=16] {'row'}, dimensions={0} | all-to-all | bytes 458752 | tf_op jit(solution)/shard_map/all_to_all | solution.py:359
  28.0 0.7 %pick.1 = (f32[32,2,1664]{2,1,0:T(2,128)S(1)}, f32[2,128]{1,0:T(2,128)S(1)}) custom-call(s32[2]{0:T(128)} %get-tuple-element.6.refs_0_.refs_3_, f32[32,2,896]{2,1,0:T(2,128)S(1)} %all_to_all.10.refs_1_), custom_call_target="tpu_custom_call" | custom-call | tf_op jit(solution)/shard_map/pick/pallas_call | solution.py:361
  28.7 19.0 %all_to_all.11.refs_0_ = f32[32,2,1664]{2,1,0:T(2,128)S(1)} all-to-all(f32[32,2,1664]{2,1,0:T(2,128)S(1)} %get-tuple-element.8), channel_id=1, replica_groups=mesh['row'=32,'col'=16] {'row'}, dimensions={0} | all-to-all | bytes 851968 | tf_op jit(solution)/shard_map/all_to_all | solution.py:368
  47.7 8.1 %step.1 = (f32[768,128]{1,0:T(8,128)}, f32[768,1536]{1,0:T(8,128)}) custom-call(f32[32,2,1664]{2,1,0:T(2,128)S(1)} %all_to_all.11.refs_0_, f32[2,128]{1,0:T(2,128)S(1)} %get-tuple-element.9.refs_1_, s32[192]{0:T(256)} %refs_2_.1, s32[2]{0:T(128)} %get-tuple-element.6.refs_0_.refs_3_, f32[6,128]{1,0:T(8,128)} %bitcast.5, f32[64,768]{1,0:T(8,128)} %bitcast.3), custom_call_target="tpu_custom_call" | custom-call | tf_op jit(solution)/shard_map/step/pallas_call | solution.py:314

commit v5 on v4

--- a/solution.py
+++ b/solution.py
@@ -13,6 +13,8 @@
 VMEM = pltpu.VMEM
 SMEM = pltpu.SMEM
 CHUNK = 256
+TASK_CHUNKS = 3
+IDLE_STEPS = 28
 DEPTH = 3 * FEAT + 16
 STEP_VMEM = 24 * 1024 * 1024
 
@@ -134,7 +136,7 @@
             for k in range(s + 2, 8):
                 c[k] = c[k] - (u * down(c[k], s) + v * down(c[k], s + 1))
             r = r - (u * row0 + v * row1)
-            upto = max(0, len(tasks) * (4 * b + s // 2 + 1 - steps // 2) // (steps // 2))
+            upto = max(0, len(tasks) * (4 * b + s // 2 + 1 - IDLE_STEPS) // (steps - IDLE_STEPS))
             for task in tasks[done:upto]:
                 task()
             done = upto
@@ -250,7 +252,7 @@
     tasks += [later(col_task, j) for j in range(tiles_across)]
     tasks += [wait_task] + [later(left_task, i) for i in range(tiles_here)]
     tasks += [later(row_task, i) for i in range(tiles_here)]
-    tasks += [later(kern_task, i, n) for n in range(cols // CHUNK) for i in range(tiles_here)]
+    tasks += [later(kern_task, i, n) for n in range(TASK_CHUNKS) for i in range(tiles_here)]
     inverse_factor(gram + pivot_noise, inv_ref, tasks)
 
     hi, lo = split2(inv_ref[...])
@@ -282,7 +284,11 @@
         for i in range(tiles_here):
             here = slice(i * TILE, (i + 1) * TILE)
             part = pl.ds(pl.multiple_of((ahead + i) * TILE, TILE), TILE)
-            out_ref[here, part] += jnp.where(diagonal, noise_ref[i : i + 1, :], 0.0)
+
+
+            @pl.when(ahead + i < TASK_CHUNKS * (CHUNK // TILE))
+            def _():
+                out_ref[here, part] += jnp.where(diagonal, noise_ref[i : i + 1, :], 0.0)
 
     copies = [panel_copy]
     per_chunk = CHUNK // TILE
@@ -291,13 +297,29 @@
         for i in range(tiles_here):
             here = slice(i * TILE, (i + 1) * TILE)
             taken = dot(row_panel_ref[here, :], col_panel_ref[:, across])
+            kern = jnp.exp(dot(left_ref[here, :], right_ref[:, across])) if n >= TASK_CHUNKS else None
             row_tile = map_ref[first_row_slot + i]
             for h in range(per_chunk):
                 col_tile = map_ref[first_col_slot + n * per_chunk + h]
                 live = (row_tile >= col_tile) & (col_tile > pivot)
                 part = slice(n * CHUNK + h * TILE, n * CHUNK + (h + 1) * TILE)
-                value = out_ref[here, part] - taken[:, h * TILE : (h + 1) * TILE]
+                value = (kern[:, h * TILE : (h + 1) * TILE] if n >= TASK_CHUNKS else out_ref[here, part]) - taken[:, h * TILE : (h + 1) * TILE]
                 out_ref[here, part] = jnp.where(live, value, 0.0)
+        if n >= TASK_CHUNKS:
+
+            @pl.when((ahead >= 0) & (ahead < tiles_across))
+            def _():
+                for h in range(per_chunk):
+                    i = n * per_chunk + h - ahead
+
+                    @pl.when((i >= 0) & (i < tiles_here))
+                    def _():
+                        here = pl.ds(pl.multiple_of(i * TILE, TILE), TILE)
+                        part = slice(n * CHUNK + h * TILE, n * CHUNK + (h + 1) * TILE)
+                        live = map_ref[first_row_slot + i] > pivot
+                        own = jnp.where(diagonal, noise_ref[pl.ds(i, 1), :], 0.0)
+                        out_ref[here, part] += jnp.where(live, own, 0.0)
+
         copy = pltpu.make_async_copy(
             out_ref.at[:, across], trailing_hbm.at[:, across], out_sems.at[1 + n]
         )

time: 56 us -> 56 us (level)
  no operation moved by 1% of the time
where the time goes in v5:
time: 56 us; the launch traced here: 55.8 us
  blocking collectives  44.1 us (79%)
  Pallas kernels  10.5 us (19%)
  between operations  1.29 us (2%)
    all_to_all x1, blocking collectives, shards(): got = lax.all_to_all(packed, 'row', 0, 0, tiled=True)  25.1 us
    all_to_all x1, blocking collectives, shards(): gathered = lax.all_to_all(picked, 'row', 0, 0, tiled=True)  19 us
    pallas_call x1, Pallas kernels, step_call(): pl.pallas_call(lambda *refs: step_kernel(tiles_here, *refs), out_shape=(s...  8.15 us
    pallas_call x1, Pallas kernels, shards(): pl.pallas_call(lambda *refs: pack_kernel(tiles_here, *refs), out_shape=(V...  1.61 us

profile of v5, /device:TPU:56, one launch (start us, length us, event | category | flops | bytes accessed | tf_op | source)
XLA Modules:
  0.0 55.8 jit_solution(5645357596640192930)
XLA Ops:
  1.3 1.6 %pack.1 = (f32[32,2,896]{2,1,0:T(2,128)S(1)}, s32[2]{0:T(128)}) custom-call(s32[192]{0:T(256)} %refs_2_.1, s32[1]{0:T(128)S(6)} %copy.6.refs_1_, f32[64,768]{1,0:T(8,128)} %bitcast.2, f32[6,128]{1,0:T(8,128)} %bitcast.4), custom_call_target="tpu_custom_call" | custom-call | tf_op jit(solution)/shard_map/pack/pallas_call | solution.py:374
  2.9 25.1 %all_to_all.10.refs_1_ = f32[32,2,896]{2,1,0:T(2,128)S(1)} all-to-all(f32[32,2,896]{2,1,0:T(2,128)S(1)} %get-tuple-element.7), channel_id=1, replica_groups=mesh['row'=32,'col'=16] {'row'}, dimensions={0} | all-to-all | bytes 458752 | tf_op jit(solution)/shard_map/all_to_all | solution.py:381
  28.0 0.7 %pick.1 = (f32[32,2,1664]{2,1,0:T(2,128)S(1)}, f32[2,128]{1,0:T(2,128)S(1)}) custom-call(s32[2]{0:T(128)} %get-tuple-element.6.refs_0_.refs_3_, f32[32,2,896]{2,1,0:T(2,128)S(1)} %all_to_all.10.refs_1_), custom_call_target="tpu_custom_call" | custom-call | tf_op jit(solution)/shard_map/pick/pallas_call | solution.py:383
  28.7 19.0 %all_to_all.11.refs_0_ = f32[32,2,1664]{2,1,0:T(2,128)S(1)} all-to-all(f32[32,2,1664]{2,1,0:T(2,128)S(1)} %get-tuple-element.8), channel_id=1, replica_groups=mesh['row'=32,'col'=16] {'row'}, dimensions={0} | all-to-all | bytes 851968 | tf_op jit(solution)/shard_map/all_to_all | solution.py:390
  47.7 8.1 %step.1 = (f32[768,128]{1,0:T(8,128)}, f32[768,1536]{1,0:T(8,128)}) custom-call(f32[32,2,1664]{2,1,0:T(2,128)S(1)} %all_to_all.11.refs_0_, f32[2,128]{1,0:T(2,128)S(1)} %get-tuple-element.9.refs_1_, s32[192]{0:T(256)} %refs_2_.1, s32[2]{0:T(128)} %get-tuple-element.6.refs_0_.refs_3_, f32[6,128]{1,0:T(8,128)} %bitcast.5, f32[64,768]{1,0:T(8,128)} %bitcast.3), custom_call_target="tpu_custom_call" | custom-call | tf_op jit(solution)/shard_map/step/pallas_call | solution.py:336
